TPU v7x, 32 devices: a whole 2x2x4 slice. The times are simulated.
32 devices in a mesh: rows: 2 (over core), tp: 4 (over y, x), attn: 4 (over z).
Axes of the slice: x: 2, y: 2, z: 4, core: 2. Of those that a mesh axis runs over, the one named last changes fastest.
Arguments:
- tokens: bfloat16 [4096, 4096], P(('rows', 'attn')), may hold values from -60 to 60, as said below
- norm_gain: bfloat16 [4096], replicated, may hold values from 0.099609375 to 1.8984375
- w_query: bfloat16 [4096, 2048], P('rows', 'tp'), may hold values from -1 to 1, as said below
- key_projection_weight: bfloat16 [4096, 512], P('rows', 'tp'), may hold values from -8 to 8, as said below
- value_projection_weight: bfloat16 [4096, 512], P('rows', 'tp'), may hold values from -0.09375 to 0.09375
- documents: int32 [2, 2048], P('rows'), may hold values from 0 to 5, never falling along the last dimension, each value on 1 to 1024 neighbouring positions
Outputs:
- attn_out: bfloat16 [4096, 2048], P(('rows', 'attn'), 'tp')
Inputs may be any that keep to these rules, and one draw needn't show every extreme that they name: `tokens`: activations of order one. `w_query`: entries of order 4096 ** -0.5. `key_projection_weight`: entries of order one or smaller. `documents`: along each window the document numbers never fall; every document spans 1 to 1024 tokens and some document of each window spans exactly 1024.
All inputs are finite; a program needn't handle non-finite values.
Results may differ from a plain program's by a relative error of at most 0.012.
The roundings to bfloat16 on the way count: a program that leaves them out, or rounds other values in their place, can miss the bound.
Values may be sent and summed in bfloat16 or wider, within the bound.
A program may use at most 64 MiB of HBM per device.

v0:
```python
import math

import jax
import jax.numpy as jnp
from jax import lax
from jax.sharding import PartitionSpec as P

HEAD_SIZE = 128


def rotary(vectors, positions):
    head_dim = vectors.shape[-1]
    half_dim = head_dim // 2
    frequency = jnp.exp(
        jnp.arange(half_dim, dtype=jnp.float32) * (-2.0 * math.log(500000.0) / head_dim)
    )
    angles = positions.astype(jnp.float32)[:, None] * frequency[None, :]
    cosine_table = jnp.cos(angles)[:, None, :]
    sine_table = jnp.sin(angles)[:, None, :]
    first_half = vectors[..., :half_dim]
    second_half = vectors[..., half_dim:]
    return jnp.concatenate(
        [
            first_half * cosine_table - second_half * sine_table,
            second_half * cosine_table + first_half * sine_table,
        ],
        axis=-1,
    )


def attend(query_piece, first_row, keys_window, values_window, doc_ids, kv_heads, head_dim):
    piece_rows = query_piece.shape[0]
    group_width = query_piece.shape[1] // (kv_heads * head_dim)
    grouped_heads = query_piece.reshape(piece_rows, kv_heads, group_width, head_dim)
    query_docs = lax.dynamic_slice_in_dim(doc_ids, first_row, piece_rows)
    query_pos = first_row + jnp.arange(piece_rows, dtype=jnp.int32)
    doc_begin = jnp.sum((doc_ids < query_docs[0]).astype(jnp.int32))
    block_low = doc_begin // piece_rows
    block_high = first_row // piece_rows + 1
    score_scale = 1.0 / math.sqrt(head_dim)

    def visit_block(block_index, carry):
        run_max, run_sum, run_acc = carry
        block_start = block_index * piece_rows
        key_block = lax.dynamic_slice_in_dim(keys_window, block_start, piece_rows, 0).reshape(
            piece_rows, kv_heads, head_dim
        )
        value_block = lax.dynamic_slice_in_dim(values_window, block_start, piece_rows, 0).reshape(
            piece_rows, kv_heads, head_dim
        )
        key_docs = lax.dynamic_slice_in_dim(doc_ids, block_start, piece_rows)
        key_pos = block_start + jnp.arange(piece_rows, dtype=jnp.int32)
        visible = (query_docs[:, None] == key_docs[None, :]) & (
            query_pos[:, None] >= key_pos[None, :]
        )
        scores = (
            jnp.einsum(
                "pcgd,jcd->cgpj", grouped_heads, key_block, preferred_element_type=jnp.float32
            )
            * score_scale
        )
        scores = jnp.where(visible, scores, -1e30)
        new_max = jnp.maximum(run_max, jnp.max(scores, axis=-1))
        factor = jnp.exp(run_max - new_max)
        weights = jnp.where(visible, jnp.exp(scores - new_max[..., None]), 0.0)
        run_sum = run_sum * factor + jnp.sum(weights, axis=-1)
        run_acc = run_acc * factor[..., None] + jnp.einsum(
            "cgpj,jcd->cgpd",
            weights.astype(jnp.bfloat16),
            value_block,
            preferred_element_type=jnp.float32,
        )
        return (new_max, run_sum, run_acc)

    initial = (
        jnp.full((kv_heads, group_width, piece_rows), -1e30, jnp.float32),
        jnp.zeros((kv_heads, group_width, piece_rows), jnp.float32),
        jnp.zeros((kv_heads, group_width, piece_rows, head_dim), jnp.float32),
    )
    run_max, run_sum, run_acc = lax.fori_loop(block_low, block_high, visit_block, initial)
    mixed_out = run_acc / run_sum[..., None]
    return (
        jnp.transpose(mixed_out, (2, 0, 1, 3))
        .reshape(piece_rows, kv_heads * group_width * head_dim)
        .astype(jnp.bfloat16)
    )


def on_device(
    tokens, norm_gain, w_query, key_projection_weight, value_projection_weight, documents
):
    tok_rows = tokens.shape[0]
    query_width = w_query.shape[1]
    kv_width = key_projection_weight.shape[1]
    widened = tokens.astype(jnp.float32)
    mean_sq = jnp.mean(widened * widened, axis=-1, keepdims=True)
    normalized_input = (
        widened * lax.rsqrt(mean_sq + 1e-05) * norm_gain.astype(jnp.float32)
    ).astype(jnp.bfloat16)

    def add_rows(shard_block):
        return jnp.dot(normalized_input, shard_block, preferred_element_type=jnp.float32)

    my_index = lax.axis_index("attn")
    attn_size = lax.axis_size("attn")
    query_proj = add_rows(lax.all_gather(w_query, "rows", axis=0, tiled=True))
    key_projected = add_rows(lax.all_gather(key_projection_weight, "rows", axis=0, tiled=True))
    value_proj = add_rows(lax.all_gather(value_projection_weight, "rows", axis=0, tiled=True))
    positions = my_index * tok_rows + jnp.arange(tok_rows, dtype=jnp.int32)
    query_vectors_all = (
        rotary(query_proj.reshape(tok_rows, query_width // HEAD_SIZE, HEAD_SIZE), positions)
        .reshape(tok_rows, query_width)
        .astype(jnp.bfloat16)
    )
    keys_local = (
        rotary(key_projected.reshape(tok_rows, kv_width // HEAD_SIZE, HEAD_SIZE), positions)
        .reshape(tok_rows, kv_width)
        .astype(jnp.bfloat16)
    )
    values_local = value_proj.astype(jnp.bfloat16)
    keys_window, values_window = (
        lax.all_gather(keys_local, "attn", axis=0, tiled=True),
        lax.all_gather(values_local, "attn", axis=0, tiled=True),
    )
    doc_ids = documents[0]
    piece_rows = tok_rows // attn_size
    kv_heads = kv_width // HEAD_SIZE
    results = []
    for piece_index in range(attn_size):
        first_row = my_index * tok_rows + piece_index * piece_rows
        query_piece = query_vectors_all[piece_index * piece_rows : (piece_index + 1) * piece_rows]
        results.append(
            attend(query_piece, first_row, keys_window, values_window, doc_ids, kv_heads, HEAD_SIZE)
        )
    return jnp.concatenate(results, axis=0)


def solution(mesh):
    placed = (
        P(("rows", "attn"), None),
        P(),
        P("rows", "tp"),
        P("rows", "tp"),
        P("rows", "tp"),
        P("rows", None),
    )
    return jax.shard_map(
        on_device, mesh=mesh, in_specs=placed, out_specs=P(("rows", "attn"), "tp"), check_vma=False
    )
```

profile of v0, /device:TPU:12, one launch (start us, length us, event | category | flops | bytes accessed | tf_op | source)
XLA Modules:
  0.0 124.8 jit_solution(16644615421658258439)
XLA Ops:
  9.5 1.4 %convert_reduce_fusion.3 = (s32[]{:T(128)}, s32[]{:T(128)}, s32[]{:T(128)}, s32[]{:T(128)}) fusion(s32[2048]{0:T(1024)} %bitcast.286, s32[]{:T(128)S(1)} %bitcast.284, s32[]{:T(128)S(1)} %bitcast.278, s32[]{:T(128)S(1)} %bitcast.280, s32[]{:T(128)S(1)} %bitcast.282), kind=kLoop, calls=%fused_computation.164 | loop fusion | flops 24572 | bytes 8224 | tf_op jit(solution)/shard_map/reduce_sum | solution.py:37
  21.3 3.1 %fusion.84 = f32[512]{0:T(512)S(1)} fusion(bf16[512,4096]{1,0:T(8,128)(2,1)} %param.14), kind=kLoop, calls=%fused_computation.114 | loop fusion | flops 6290944 | bytes 4196352 | tf_op jit(solution)/shard_map/reduce_sum | solution.py:96
  24.4 1.8 %multiply_cosine_fusion = (f32[512,64]{1,0:T(8,128)S(1)}, f32[512,64]{1,0:T(8,128)}) fusion(f32[64]{0:T(128)S(1)} %multiply_exponential_fusion, f32[512]{0:T(512)S(1)} %add_convert_fusion.1), kind=kLoop, calls=%fused_computation.129 | loop fusion | flops 32768 | bytes 264448 | tf_op jit(solution)/shard_map/cos | solution.py:18
  26.2 4.2 %convolution_bitcast_fusion.4 = f32[512,1,128]{0,2,1:T(8,128)S(1)} fusion(bf16[4096,128]{1,0:T(8,128)(2,1)} %all-gather.5.cloned.1.call-done, bf16[512,4096]{1,0:T(8,128)(2,1)} %param.14, f32[4096]{0:T(1024)S(1)} %convert_element_type.88, f32[512]{0:T(512)S(1)} %add_rsqrt_fusion), kind=kOutput, calls=%fused_computation.117 | convolution fusion | flops 545259520 | bytes 5523456 | tf_op jit(solution)/shard_map/dot_general | solution.py:102
  31.0 16.5 %all-gather = bf16[2048,1,128]{0,2,1:T(8,128)(2,1)S(1)} all-gather(bf16[512,1,128]{0,2,1:T(8,128)(2,1)S(1)} %pad_maximum_fusion.2), channel_id=2, replica_groups=mesh['rows'=2,'tp'=4,'attn'=4] {'attn'}, dimensions={0}, use_global_device_ids=true | all-gather | bytes 655360 | tf_op jit(solution)/shard_map/all_gather | solution.py:122
  47.9 3.8 %convolution_convert_fusion = bf16[512,128]{1,0:T(8,128)(2,1)S(1)} fusion(bf16[4096,128]{1,0:T(8,128)(2,1)} %all-gather.9.cloned.1.call-done, bf16[512,4096]{1,0:T(8,128)(2,1)} %param.14, f32[4096]{0:T(1024)S(1)} %convert_element_type.88, f32[512]{0:T(512)S(1)} %add_rsqrt_fusion), kind=kOutput, calls=%fused_computation.118 | convolution fusion | flops 545325056 | bytes 5392384 | tf_op jit(solution)/shard_map/dot_general | solution.py:102
  51.6 14.9 %all_gather.19 = bf16[2048,128]{1,0:T(8,128)(2,1)S(1)} all-gather(bf16[512,128]{1,0:T(8,128)(2,1)S(1)} %convolution_convert_fusion), channel_id=1, replica_groups=mesh['rows'=2,'tp'=4,'attn'=4] {'attn'}, dimensions={0}, use_global_device_ids=true | all-gather | bytes 655360 | tf_op jit(solution)/shard_map/all_gather | solution.py:123
  66.6 5.9 %fusion.107 = f32[512,512]{0,1:T(8,128)S(1)} fusion(bf16[4096,512]{1,0:T(8,128)(2,1)} %all-gather.7.cloned.1.call-done, bf16[512,4096]{1,0:T(8,128)(2,1)} %param.14, f32[4096]{0:T(1024)S(1)} %convert_element_type.88, f32[512]{0:T(512)S(1)} %add_rsqrt_fusion), kind=kOutput, calls=%fused_computation.172 | convolution fusion | flops 2155872256 | bytes 9455616 | tf_op jit(solution)/shard_map/dot_general | solution.py:102
  72.5 0.9 fusion.114
  73.7 1.4 %copy.26 = f32[512,4,64]{2,0,1:T(8,128)S(1)} copy(f32[512,4,64]{0,2,1:T(8,128)} %get-tuple-element.519) | data formatting | bytes 1048576
  75.1 1.2 subtract_convert_fusion
  76.7 7.6 %while.60 = (s32[]{:T(128)}, f32[1,4,128]{2,1,0:T(4,128)S(1)}, f32[1,4,128]{2,1,0:T(4,128)S(1)}, f32[1,4,128,128]{3,2,1,0:T(8,128)S(1)}, s32[]{:T(128)}, /*index...) while((s32[]{:T(128)}, f32[1,4,128]{2,1,0:T(4,128)S(1)}, ...), condition=%wide.region_5.6_spmd.clone, body=%wide.region_2.5_spmd.clone.sunk | while | flops 34326276 | bytes 1609935 | solution.py:80
  81.3 0.8 dynamic_slice.134
  84.6 9.1 %while.61 = (s32[]{:T(128)}, f32[1,4,128]{2,1,0:T(4,128)S(1)}, f32[1,4,128]{2,1,0:T(4,128)S(1)}, f32[1,4,128,128]{3,2,1,0:T(8,128)S(1)}, s32[]{:T(128)}, /*index...) while((s32[]{:T(128)}, f32[1,4,128]{2,1,0:T(4,128)S(1)}, ...), condition=%wide.region_10.11_spmd.clone, body=%wide.region_7.10_spmd.clone.sunk | while | flops 34326276 | bytes 1609935 | solution.py:80
  87.7 0.8 dynamic_slice.137
  94.0 10.6 %while.62 = (s32[]{:T(128)}, f32[1,4,128]{2,1,0:T(4,128)S(1)}, f32[1,4,128]{2,1,0:T(4,128)S(1)}, f32[1,4,128,128]{3,2,1,0:T(8,128)S(1)}, s32[]{:T(128)}, /*index...) while((s32[]{:T(128)}, f32[1,4,128]{2,1,0:T(4,128)S(1)}, ...), condition=%wide.region_15.16_spmd.clone, body=%wide.region_12.15_spmd.clone.sunk | while | flops 34326276 | bytes 1609935 | solution.py:80
  97.1 0.8 dynamic_slice.140
  103.2 0.8 dynamic_slice.140
  105.0 12.2 %while.63 = (s32[]{:T(128)}, f32[1,4,128]{2,1,0:T(4,128)S(1)}, f32[1,4,128]{2,1,0:T(4,128)S(1)}, f32[1,4,128,128]{3,2,1,0:T(8,128)S(1)}, s32[]{:T(128)}, /*index...) while((s32[]{:T(128)}, f32[1,4,128]{2,1,0:T(4,128)S(1)}, ...), condition=%wide.region_20.21_spmd.clone, body=%wide.region_17.20_spmd.clone.sunk | while | flops 34326276 | bytes 1609935 | solution.py:80
  106.5 0.8 dynamic_slice.143
  108.1 0.8 dynamic_slice.143
  111.1 0.8 dynamic_slice.143
  112.6 0.8 dynamic_slice.143
  117.5 0.8 pad_maximum_fusion
  (267 shorter events, 38.0 us)
Async XLA Ops:
  6.5 19.7 %all-gather.5.cloned.1.call-start = ((), (), s32[]{:S(2)}) async-start(), calls=%async_computation | async-start | bytes 1572864 | tf_op jit(solution)/shard_map/all_gather | solution.py:107
  7.3 40.6 %all-gather.9.cloned.1.call-start = ((), (), s32[]{:S(2)}) async-start(), calls=%async_computation.2 | async-start | bytes 1572864 | tf_op jit(solution)/shard_map/all_gather | solution.py:108
  8.0 58.6 %all-gather.7.cloned.1.call-start = ((), (), s32[]{:S(2)}) async-start(), calls=%async_computation.1 | async-start | bytes 6291456 | tf_op jit(solution)/shard_map/all_gather | solution.py:106
Sparse Core Ops, SparseCore 0:
  8.9 10.3 all-gather.4
  20.9 10.1 all-gather.8
  32.6 14.8 all-gather.6
where the time goes:
time: 124 us; the launch traced here: 125 us
  blocking collectives  31.4 us (25%)
  matrix products  26.8 us (22%)
  local copies, waits for them, and re-layouts  24.1 us (19%)
  between operations  23.1 us (19%)
  other arithmetic  15.6 us (13%)
  waiting for transfers between devices  2.11 us (2%)
  loops' own time  1.65 us (1%)
    dynamic_slice x26, local copies, waits for them, and re-layouts, visit_block(): key_docs = lax.dynamic_slice_in_dim(doc_ids, block_start, piece_rows)  19.9 us
    all_gather x1, blocking collectives, on_device(): lax.all_gather(keys_local, 'attn', axis=0, tiled=True)  16.5 us
    all_gather x1, blocking collectives, on_device(): lax.all_gather(values_local, 'attn', axis=0, tiled=True)  14.9 us
    dot_general x3, matrix products, add_rows(): jnp.dot(normalized_input, shard_block, preferred_element_type=jnp.float32)  14 us
    dot_general x26, matrix products, visit_block(): jnp.einsum('cgpj,jcd->cgpd', weights.astype(jnp.bfloat16), value_block, p...  7.39 us
    dot_general x26, matrix products, visit_block(): jnp.einsum('pcgd,jcd->cgpj', grouped_heads, key_block, preferred_element_...  5.4 us
    reduce_sum x1, other arithmetic, on_device(): mean_sq = jnp.mean(widened * widened, axis=-1, keepdims=True)  3.08 us
    and x26, other arithmetic, visit_block(): (query_docs[:, None] == key_docs[None, :]) & (query_pos[:, None] >= key_p...  2.67 us
  transfers between devices with their start and end apart: 3, of which 0 were waited for; matrix products, arithmetic and copies ran while one was open for 13% of the time, Pallas kernels for 0%

commit v1 on v0

v1 whole, which is shorter than its diff:
```python
import functools
import math

import jax
import jax.numpy as jnp
import numpy as np
from jax import lax
from jax.experimental import pallas as pl
from jax.experimental.pallas import tpu as pltpu
from jax.sharding import PartitionSpec as P

HEAD = 128
MOST = 1024
TQ = 128
BF16 = jnp.bfloat16
F32 = jnp.float32
MESH = pl.DeviceIdType.MESH


def rotary_table(window):
    half = HEAD // 2
    frequency = np.exp(
        np.arange(half, dtype=np.float32) * np.float32(-2.0 * math.log(500000.0) / HEAD)
    ).astype(np.float32)
    angles = np.arange(window, dtype=np.float32)[:, None] * frequency[None, :]
    return np.concatenate([np.cos(angles), np.sin(angles)], axis=1).astype(np.float32)


def kernel(
    n_rows, n_attn, back, chunk,
    tok, gain, wq, wk, wv, docs, table, out,
    xt, xn, wkv_buf, wq_buf, kv, q, tab, kdoc, qdoc,
    tok_sem, own_sem, w_send, w_recv, kv_send, kv_recv,
):
    rows = tok.shape[0]
    depth = wk.shape[0]
    kvw = wk.shape[1]
    qw = wq.shape[1]
    kv_heads = kvw // HEAD
    group = qw // kvw
    chunks = rows // chunk
    tiles = rows // TQ
    mine = back * rows
    span = min(mine + rows, -(-(MOST - 1 + TQ) // TQ) * TQ)
    me = lax.axis_index("rows")
    at = lax.axis_index("attn")

    tok_copies = [
        pltpu.make_async_copy(
            tok.at[pl.ds(c * chunk, chunk)], xt.at[pl.ds(c * chunk, chunk)], tok_sem.at[c]
        )
        for c in range(chunks)
    ]
    own_copies = [
        pltpu.make_async_copy(wk, wkv_buf.at[0, :, pl.ds(0, kvw)], own_sem.at[0]),
        pltpu.make_async_copy(wv, wkv_buf.at[0, :, pl.ds(kvw, kvw)], own_sem.at[1]),
        pltpu.make_async_copy(wq, wq_buf.at[0], own_sem.at[2]),
        pltpu.make_async_copy(
            table.at[pl.ds(pl.multiple_of(at * rows, rows), rows)], tab, own_sem.at[3]
        ),
    ]
    tok_copies[0].start()
    own_copies[0].start()
    own_copies[1].start()
    for copy in tok_copies[1:]:
        copy.start()
    own_copies[3].start()
    own_copies[2].start()

    barrier = pltpu.get_barrier_semaphore()
    for d in range(1, n_rows):
        pl.semaphore_signal(
            barrier, inc=1, device_id={"rows": lax.rem(me + d, n_rows)}, device_id_type=MESH
        )
    has_prev = at > 0
    has_next = at < n_attn - 1
    if back:

        @pl.when(has_prev)
        def _():
            pl.semaphore_signal(
                barrier, inc=1, device_id={"attn": at - 1}, device_id_type=MESH
            )

        @pl.when(has_next)
        def _():
            pl.semaphore_signal(
                barrier, inc=1, device_id={"attn": at + 1}, device_id_type=MESH
            )

        pl.semaphore_wait(
            barrier, n_rows - 1 + has_prev.astype(jnp.int32) + has_next.astype(jnp.int32)
        )
    elif n_rows > 1:
        pl.semaphore_wait(barrier, n_rows - 1)

    def weight_copy(d, which):
        src, dst = (
            (wk, wkv_buf.at[d, :, pl.ds(0, kvw)]),
            (wv, wkv_buf.at[d, :, pl.ds(kvw, kvw)]),
            (wq, wq_buf.at[d]),
        )[which]
        return pltpu.make_async_remote_copy(
            src_ref=src, dst_ref=dst,
            send_sem=w_send.at[d, which], recv_sem=w_recv.at[d, which],
            device_id={"rows": lax.rem(me + d, n_rows)}, device_id_type=MESH,
        )

    for which in range(3):
        for d in range(1, n_rows):
            weight_copy(d, which).start()

    for s in range(back + 1):
        block = at - back + s
        keep = pl.multiple_of(jnp.maximum(block, 0) * rows, rows)
        kdoc[:, pl.ds(s * rows, rows)] = jnp.where(block >= 0, docs[:, pl.ds(keep, rows)], -1)
    for t in range(tiles):
        row = kdoc[:, pl.ds(mine + t * TQ, TQ)]
        qdoc[pl.ds(t * TQ, TQ), :] = jnp.broadcast_to(row, (TQ, TQ)).T
    for s in range(back):

        @pl.when(at - back + s < 0)
        def _():
            kv[pl.ds(s * rows, rows), :] = jnp.zeros((rows, 2 * kvw), BF16)

    lane = lax.broadcasted_iota(jnp.int32, (1, HEAD), 1)

    def tables(start, size):
        t = tab[pl.ds(start, size), :]
        swapped = pltpu.roll(t, HEAD // 2, 1)
        low = lane < HEAD // 2
        return jnp.where(low, t, swapped), jnp.where(low, -swapped, t)

    def rotate(u, cosine, sine):
        return (u * cosine + pltpu.roll(u, HEAD // 2, 1) * sine).astype(BF16)

    def project(start, size, weights):
        total = None
        for d in range(n_rows):
            owner = lax.rem(me - d + n_rows, n_rows)
            part = jnp.dot(
                xn[pl.ds(start, size), pl.ds(pl.multiple_of(owner * depth, depth), depth)],
                weights[d],
                preferred_element_type=F32,
            )
            total = part if total is None else total + part
        return total

    def hop(s, c):
        return pltpu.make_async_remote_copy(
            src_ref=kv.at[pl.ds((back - s) * rows + c * chunk, chunk)],
            dst_ref=kv.at[pl.ds((back - s - 1) * rows + c * chunk, chunk)],
            send_sem=kv_send.at[s, c], recv_sem=kv_recv.at[s, c],
            device_id={"attn": jnp.minimum(at + 1, n_attn - 1)}, device_id_type=MESH,
        )

    strip = 16
    for c in range(chunks):
        tok_copies[c].wait()

        @pl.loop(0, chunk // strip)
        def _(i):
            here = pl.ds(pl.multiple_of(c * chunk + i * strip, strip), strip)
            x = xt[here, :].astype(F32)
            scale = lax.rsqrt(jnp.mean(x * x, axis=-1, keepdims=True) + 1e-05)
            xn[here, :] = (x * scale * gain[...].astype(F32)).astype(BF16)

        if c == 0:
            own_copies[0].wait()
            own_copies[1].wait()
            own_copies[3].wait()
            for d in range(1, n_rows):
                weight_copy(d, 0).wait()
                weight_copy(d, 1).wait()
        total = project(c * chunk, chunk, wkv_buf)
        cosine, sine = tables(c * chunk, chunk)
        here = pl.ds(mine + c * chunk, chunk)
        for h in range(kv_heads):
            kv[here, pl.ds(h * HEAD, HEAD)] = rotate(
                total[:, h * HEAD : (h + 1) * HEAD], cosine, sine
            )
        kv[here, pl.ds(kvw, kvw)] = total[:, kvw:].astype(BF16)
        if back:

            @pl.when(has_next)
            def _():
                hop(0, c).start()

    own_copies[2].wait()
    for d in range(1, n_rows):
        weight_copy(d, 2).wait()
    for c in range(chunks):
        total = project(c * chunk, chunk, wq_buf)
        cosine, sine = tables(c * chunk, chunk)
        for h in range(kv_heads):
            for g in range(group):
                col = (h * group + g) * HEAD
                u = rotate(total[:, col : col + HEAD], cosine, sine)
                for t in range(chunk // TQ):
                    q[c * (chunk // TQ) + t, h, pl.ds(g * TQ, TQ), :] = u[
                        t * TQ : (t + 1) * TQ
                    ]

    for s in range(back):
        for c in range(chunks):

            @pl.when(at > s)
            def _():
                hop(s, c).wait_recv()

            if s + 1 < back:

                @pl.when((at > s) & has_next)
                def _():
                    hop(s + 1, c).start()

    factor = math.log2(math.e) / math.sqrt(HEAD)

    @pl.loop(0, tiles)
    def _(t):
        first = pl.multiple_of(t * TQ, TQ)
        begin = pl.multiple_of(jnp.maximum(mine + first + TQ - span, 0), TQ)
        query_at = lax.broadcasted_iota(jnp.int32, (TQ, 1), 0) + (mine + first)
        key_at = lax.broadcasted_iota(jnp.int32, (1, span), 1) + begin
        visible = (qdoc[pl.ds(first, TQ), :][:, :1] == kdoc[:, pl.ds(begin, span)]) & (
            query_at >= key_at
        )
        for h in range(kv_heads):
            keys = kv[pl.ds(begin, span), pl.ds(h * HEAD, HEAD)]
            vals = kv[pl.ds(begin, span), pl.ds(kvw + h * HEAD, HEAD)]
            for g in range(group):
                s = lax.dot_general(
                    q[t, h, pl.ds(g * TQ, TQ), :], keys, (((1,), (1,)), ((), ())),
                    preferred_element_type=F32,
                )
                s = jnp.where(visible, s, -1e30)
                p = jnp.exp2((s - jnp.max(s, axis=-1, keepdims=True)) * factor)
                total = jnp.sum(p, axis=-1, keepdims=True)
                mixed = jnp.dot(p.astype(BF16), vals, preferred_element_type=F32)
                out[pl.ds(first, TQ), pl.ds((h * group + g) * HEAD, HEAD)] = (
                    mixed / total
                ).astype(BF16)

    for s in range(back):
        for c in range(chunks):

            @pl.when((at >= s) & has_next)
            def _():
                hop(s, c).wait_send()


def solution(mesh):
    n_rows = mesh.shape["rows"]
    n_attn = mesh.shape["attn"]

    def on_device(tokens, norm_gain, w_query, w_key, w_value, documents):
        rows, width = tokens.shape
        depth, qw = w_query.shape
        kvw = w_key.shape[1]
        back = min(n_attn - 1, -(-(MOST - 1) // rows))
        chunk = min(rows, 256)
        chunks = rows // chunk
        table = jnp.asarray(rotary_table(documents.shape[1]))
        anywhere = pl.BlockSpec(memory_space=pl.ANY)
        vmem = pl.BlockSpec(memory_space=pltpu.VMEM)
        keys = (back + 1) * rows
        group = qw // kvw
        return pl.pallas_call(
            functools.partial(kernel, n_rows, n_attn, back, chunk),
            out_shape=jax.ShapeDtypeStruct((rows, qw), BF16),
            in_specs=[anywhere, vmem, anywhere, anywhere, anywhere, vmem, anywhere],
            out_specs=vmem,
            scratch_shapes=[
                pltpu.VMEM((rows, width), BF16),
                pltpu.VMEM((rows, width), BF16),
                pltpu.VMEM((n_rows, depth, 2 * kvw), BF16),
                pltpu.VMEM((n_rows, depth, qw), BF16),
                pltpu.VMEM((keys, 2 * kvw), BF16),
                pltpu.VMEM((rows // TQ, kvw // HEAD, group * TQ, HEAD), BF16),
                pltpu.VMEM((rows, HEAD), F32),
                pltpu.VMEM((1, keys), jnp.int32),
                pltpu.VMEM((rows, TQ), jnp.int32),
                pltpu.SemaphoreType.DMA((chunks,)),
                pltpu.SemaphoreType.DMA((4,)),
                pltpu.SemaphoreType.DMA((n_rows, 3)),
                pltpu.SemaphoreType.DMA((n_rows, 3)),
                pltpu.SemaphoreType.DMA((max(back, 1), chunks)),
                pltpu.SemaphoreType.DMA((max(back, 1), chunks)),
            ],
            compiler_params=pltpu.CompilerParams(
                collective_id=0, has_side_effects=True, vmem_limit_bytes=60 << 20
            ),
            name="layer",
        )(tokens, norm_gain.reshape(1, width), w_query, w_key, w_value, documents, table)

    placed = (
        P(("rows", "attn"), None),
        P(),
        P("rows", "tp"),
        P("rows", "tp"),
        P("rows", "tp"),
        P("rows", None),
    )
    return jax.shard_map(
        on_device, mesh=mesh, in_specs=placed, out_specs=P(("rows", "attn"), "tp"), check_vma=False
    )
```

time: 124 us -> 31.7 us (0.26)
  the two profiles are of different devices: /device:TPU:12 before, /device:TPU:18 now
where the time goes in v1:
time: 31.7 us; the launch traced here: 31.4 us
  Pallas kernels  28.2 us (89%)
  local copies, waits for them, and re-layouts  3.18 us (10%)
    pallas_call x1, Pallas kernels, on_device(): pl.pallas_call(functools.partial(kernel, n_rows, n_attn, back, chunk), ou...  28.2 us
    unnamed x1, local copies, waits for them, and re-layouts  1.87 us
    reshape x1, local copies, waits for them, and re-layouts, on_device(): norm_gain.reshape(1, width)  1.31 us

profile of v1, /device:TPU:18, one launch (start us, length us, event | category | flops | bytes accessed | tf_op | source)
XLA Modules:
  0.0 31.4 jit_solution(12552131157393039783)
XLA Ops:
  0.0 1.3 %reshape.3.gain = bf16[1,4096]{1,0:T(2,128)(2,1)} reshape(bf16[4096]{0:T(1024)(128)(2,1)} %param.8) | data formatting | bytes 16384 | tf_op jit(solution)/shard_map/reshape | solution.py:294
  1.3 28.2 %layer.1 = bf16[512,512]{1,0:T(8,128)(2,1)} custom-call(bf16[512,4096]{1,0:T(8,128)(2,1)} %tok.1, bf16[1,4096]{1,0:T(2,128)(2,1)} %reshape.3.gain, bf16[2048,512]{1,0:T(8,128)(2,1)} %wq.1, bf16[2048,128]{1,0:T(8,128)(2,1)} %wk.1, bf16[2048,128]{1,0:T(8,128)(2,1)} %wv.1, s32[1,2048]{1,0:T(1,128)} %docs.1, f32[2048,128]{1,0:T(8,128)} %constant.2.clone.table), custom_call_target="tpu_custom_call" | custom-call | tf_op jit(solution)/shard_map/layer/pallas_call | solution.py:268
  29.5 1.9 %copy.9 = bf16[512,512]{1,0:T(8,128)(2,1)} copy(bf16[512,512]{1,0:T(8,128)(2,1)} %layer.1) | data formatting | bytes 1048576

commit v2 on v1

--- a/solution.py
+++ b/solution.py
@@ -59,13 +59,12 @@
             table.at[pl.ds(pl.multiple_of(at * rows, rows), rows)], tab, own_sem.at[3]
         ),
     ]
-    tok_copies[0].start()
+    tok_copies[-1].start()
     own_copies[0].start()
     own_copies[1].start()
-    for copy in tok_copies[1:]:
+    own_copies[3].start()
+    for copy in tok_copies[-2::-1]:
         copy.start()
-    own_copies[3].start()
-    own_copies[2].start()
 
     barrier = pltpu.get_barrier_semaphore()
     for d in range(1, n_rows):
@@ -109,6 +108,7 @@
     for which in range(3):
         for d in range(1, n_rows):
             weight_copy(d, which).start()
+    own_copies[2].start()
 
     for s in range(back + 1):
         block = at - back + s
@@ -154,18 +154,29 @@
             device_id={"attn": jnp.minimum(at + 1, n_attn - 1)}, device_id_type=MESH,
         )
 
+    def arrived(s, c):
+        @pl.when(at > s)
+        def _():
+            hop(s, c).wait_recv()
+
+        if s + 1 < back:
+
+            @pl.when((at > s) & has_next)
+            def _():
+                hop(s + 1, c).start()
+
     strip = 16
-    for c in range(chunks):
+    for c in reversed(range(chunks)):
         tok_copies[c].wait()
 
-        @pl.loop(0, chunk // strip)
+        @pl.loop(0, chunk // strip, unroll=2)
         def _(i):
             here = pl.ds(pl.multiple_of(c * chunk + i * strip, strip), strip)
             x = xt[here, :].astype(F32)
             scale = lax.rsqrt(jnp.mean(x * x, axis=-1, keepdims=True) + 1e-05)
-            xn[here, :] = (x * scale * gain[...].astype(F32)).astype(BF16)
-
-        if c == 0:
+            xn[here, :] = (x * scale * gain[...].astype(F32).reshape(1, -1)).astype(BF16)
+
+        if c == chunks - 1:
             own_copies[0].wait()
             own_copies[1].wait()
             own_copies[3].wait()
@@ -186,40 +197,36 @@
             def _():
                 hop(0, c).start()
 
+    relayed = [(s, c) for s in range(back - 1) for c in reversed(range(chunks))]
+    last = [(back - 1, c) for c in reversed(range(chunks))] if back else []
+
     own_copies[2].wait()
     for d in range(1, n_rows):
         weight_copy(d, 2).wait()
-    for c in range(chunks):
-        total = project(c * chunk, chunk, wq_buf)
-        cosine, sine = tables(c * chunk, chunk)
+    part = min(rows, 2 * chunk)
+    for step in reversed(range(rows // part)):
+        for _ in range(min(1, len(relayed))):
+            arrived(*relayed.pop(0))
+        total = project(step * part, part, wq_buf)
+        cosine, sine = tables(step * part, part)
         for h in range(kv_heads):
             for g in range(group):
                 col = (h * group + g) * HEAD
                 u = rotate(total[:, col : col + HEAD], cosine, sine)
-                for t in range(chunk // TQ):
-                    q[c * (chunk // TQ) + t, h, pl.ds(g * TQ, TQ), :] = u[
+                for t in range(part // TQ):
+                    q[step * (part // TQ) + t, h, pl.ds(g * TQ, TQ), :] = u[
                         t * TQ : (t + 1) * TQ
                     ]
-
-    for s in range(back):
-        for c in range(chunks):
-
-            @pl.when(at > s)
-            def _():
-                hop(s, c).wait_recv()
-
-            if s + 1 < back:
-
-                @pl.when((at > s) & has_next)
-                def _():
-                    hop(s + 1, c).start()
+    for event in relayed:
+        arrived(*event)
 
     factor = math.log2(math.e) / math.sqrt(HEAD)
 
-    @pl.loop(0, tiles)
-    def _(t):
-        first = pl.multiple_of(t * TQ, TQ)
-        begin = pl.multiple_of(jnp.maximum(mine + first + TQ - span, 0), TQ)
+    for t in reversed(range(tiles)):
+        first = t * TQ
+        begin = max(mine + first + TQ - span, 0)
+        while last and (last[0][1] + 1) * chunk > begin:
+            arrived(*last.pop(0))
         query_at = lax.broadcasted_iota(jnp.int32, (TQ, 1), 0) + (mine + first)
         key_at = lax.broadcasted_iota(jnp.int32, (1, span), 1) + begin
         visible = (qdoc[pl.ds(first, TQ), :][:, :1] == kdoc[:, pl.ds(begin, span)]) & (
@@ -228,18 +235,20 @@
         for h in range(kv_heads):
             keys = kv[pl.ds(begin, span), pl.ds(h * HEAD, HEAD)]
             vals = kv[pl.ds(begin, span), pl.ds(kvw + h * HEAD, HEAD)]
+            s = lax.dot_general(
+                q[t, h], keys, (((1,), (1,)), ((), ())), preferred_element_type=F32
+            )
+            s = jnp.where(visible[None], s.reshape(group, TQ, span), -1e30)
+            p = jnp.exp2((s - jnp.max(s, axis=-1, keepdims=True)) * factor)
+            total = jnp.sum(p, axis=-1, keepdims=True)
+            mixed = jnp.dot(
+                p.astype(BF16).reshape(group * TQ, span), vals, preferred_element_type=F32
+            )
+            mixed = (mixed.reshape(group, TQ, HEAD) / total).astype(BF16)
             for g in range(group):
-                s = lax.dot_general(
-                    q[t, h, pl.ds(g * TQ, TQ), :], keys, (((1,), (1,)), ((), ())),
-                    preferred_element_type=F32,
-                )
-                s = jnp.where(visible, s, -1e30)
-                p = jnp.exp2((s - jnp.max(s, axis=-1, keepdims=True)) * factor)
-                total = jnp.sum(p, axis=-1, keepdims=True)
-                mixed = jnp.dot(p.astype(BF16), vals, preferred_element_type=F32)
-                out[pl.ds(first, TQ), pl.ds((h * group + g) * HEAD, HEAD)] = (
-                    mixed / total
-                ).astype(BF16)
+                out[pl.ds(first, TQ), pl.ds((h * group + g) * HEAD, HEAD)] = mixed[g]
+    for event in last:
+        arrived(*event)
 
     for s in range(back):
         for c in range(chunks):
@@ -258,7 +267,7 @@
         depth, qw = w_query.shape
         kvw = w_key.shape[1]
         back = min(n_attn - 1, -(-(MOST - 1) // rows))
-        chunk = min(rows, 256)
+        chunk = min(rows, TQ)
         chunks = rows // chunk
         table = jnp.asarray(rotary_table(documents.shape[1]))
         anywhere = pl.BlockSpec(memory_space=pl.ANY)
@@ -291,7 +300,7 @@
                 collective_id=0, has_side_effects=True, vmem_limit_bytes=60 << 20
             ),
             name="layer",
-        )(tokens, norm_gain.reshape(1, width), w_query, w_key, w_value, documents, table)
+        )(tokens, norm_gain, w_query, w_key, w_value, documents, table)
 
     placed = (
         P(("rows", "attn"), None),

time: 31.7 us -> 24.6 us (0.78)
  Pallas kernels: 28.2 us -> 22.5 us
  local copies, waits for them, and re-layouts: 3.18 us -> 1.87 us
    pallas_call x1, Pallas kernels: 28.2 us -> 22.5 us  [on_device(): pl.pallas_call(functools.partial(kernel, n_rows, n_attn, back, chunk), ou...]
    reshape x1 -> x0, local copies, waits for them, and re-layouts: 1.31 us -> none  [on_device(): norm_gain.reshape(1, width)]
where the time goes in v2:
time: 24.6 us; the launch traced here: 24.4 us
  Pallas kernels  22.5 us (91%)
  local copies, waits for them, and re-layouts  1.87 us (8%)
    pallas_call x1, Pallas kernels, on_device(): pl.pallas_call(functools.partial(kernel, n_rows, n_attn, back, chunk), ou...  22.5 us
    unnamed x1, local copies, waits for them, and re-layouts  1.87 us

profile of v2, /device:TPU:18, one launch (start us, length us, event | category | flops | bytes accessed | tf_op | source)
XLA Modules:
  0.0 24.4 jit_solution(12840390333135195090)
XLA Ops:
  0.0 22.5 %layer.1 = bf16[512,512]{1,0:T(8,128)(2,1)} custom-call(bf16[512,4096]{1,0:T(8,128)(2,1)} %tok.1, bf16[4096]{0:T(1024)(128)(2,1)} %gain.1, bf16[2048,512]{1,0:T(8,128)(2,1)} %wq.1, bf16[2048,128]{1,0:T(8,128)(2,1)} %wk.1, bf16[2048,128]{1,0:T(8,128)(2,1)} %wv.1, s32[1,2048]{1,0:T(1,128)} %docs.1, f32[2048,128]{1,0:T(8,128)} %constant.2.clone.table), custom_call_target="tpu_custom_call" | custom-call | tf_op jit(solution)/shard_map/layer/pallas_call | solution.py:277
  22.5 1.9 %copy.9 = bf16[512,512]{1,0:T(8,128)(2,1)} copy(bf16[512,512]{1,0:T(8,128)(2,1)} %layer.1) | data formatting | bytes 1048576

commit v3 on v2

--- a/solution.py
+++ b/solution.py
@@ -27,9 +27,9 @@
 
 
 def kernel(
-    n_rows, n_attn, back, chunk,
+    n_rows, n_attn, back, chunk, span,
     tok, gain, wq, wk, wv, docs, table, out,
-    xt, xn, wkv_buf, wq_buf, kv, q, tab, kdoc, qdoc,
+    probs, gains, xt, xn, wkv_buf, wq_buf, kv, q, tab, kdoc, qdoc,
     tok_sem, own_sem, w_send, w_recv, kv_send, kv_recv,
 ):
     rows = tok.shape[0]
@@ -41,7 +41,6 @@
     chunks = rows // chunk
     tiles = rows // TQ
     mine = back * rows
-    span = min(mine + rows, -(-(MOST - 1 + TQ) // TQ) * TQ)
     me = lax.axis_index("rows")
     at = lax.axis_index("attn")
 
@@ -93,22 +92,35 @@
     elif n_rows > 1:
         pl.semaphore_wait(barrier, n_rows - 1)
 
-    def weight_copy(d, which):
+    cuts = 1
+    cut = depth // cuts
+
+    def weight_copies(d, which):
         src, dst = (
             (wk, wkv_buf.at[d, :, pl.ds(0, kvw)]),
             (wv, wkv_buf.at[d, :, pl.ds(kvw, kvw)]),
             (wq, wq_buf.at[d]),
         )[which]
-        return pltpu.make_async_remote_copy(
-            src_ref=src, dst_ref=dst,
-            send_sem=w_send.at[d, which], recv_sem=w_recv.at[d, which],
-            device_id={"rows": lax.rem(me + d, n_rows)}, device_id_type=MESH,
-        )
+        return [
+            pltpu.make_async_remote_copy(
+                src_ref=src.at[pl.ds(k * cut, cut)], dst_ref=dst.at[pl.ds(k * cut, cut)],
+                send_sem=w_send.at[d, which, k], recv_sem=w_recv.at[d, which, k],
+                device_id={"rows": lax.rem(me + d, n_rows)}, device_id_type=MESH,
+            )
+            for k in range(cuts)
+        ]
+
+    def start_weights(d, which):
+        for copy in weight_copies(d, which):
+            copy.start()
+
+    def wait_weights(d, which):
+        for copy in weight_copies(d, which):
+            copy.wait()
 
     for which in range(3):
         for d in range(1, n_rows):
-            weight_copy(d, which).start()
-    own_copies[2].start()
+            start_weights(d, which)
 
     for s in range(back + 1):
         block = at - back + s
@@ -140,7 +152,7 @@
             owner = lax.rem(me - d + n_rows, n_rows)
             part = jnp.dot(
                 xn[pl.ds(start, size), pl.ds(pl.multiple_of(owner * depth, depth), depth)],
-                weights[d],
+                weights(d),
                 preferred_element_type=F32,
             )
             total = part if total is None else total + part
@@ -165,27 +177,43 @@
             def _():
                 hop(s + 1, c).start()
 
-    strip = 16
+    half = min(rows, 2 * chunk)
+    q_rows = rows
+    strip, piece = 16, 256
+    width = tok.shape[1]
+    gains[...] = jnp.broadcast_to(gain[...].astype(F32).reshape(1, -1), gains.shape)
     for c in reversed(range(chunks)):
         tok_copies[c].wait()
 
-        @pl.loop(0, chunk // strip, unroll=2)
+        @pl.loop(0, chunk // strip, unroll=4)
         def _(i):
             here = pl.ds(pl.multiple_of(c * chunk + i * strip, strip), strip)
-            x = xt[here, :].astype(F32)
-            scale = lax.rsqrt(jnp.mean(x * x, axis=-1, keepdims=True) + 1e-05)
-            xn[here, :] = (x * scale * gain[...].astype(F32).reshape(1, -1)).astype(BF16)
+            squares = jnp.zeros((strip, piece), F32)
+            for k in range(width // piece):
+                x = xt[here, pl.ds(k * piece, piece)].astype(F32)
+                squares = squares + x * x
+            mean_sq = jnp.sum(squares, axis=-1, keepdims=True) * (1.0 / width)
+            scale = jnp.broadcast_to(lax.rsqrt(mean_sq + 1e-05), (strip, piece))
+            for k in range(width // piece):
+                cols = pl.ds(k * piece, piece)
+                x = xt[here, cols].astype(F32) * scale
+                xn[here, cols] = (
+                    x.reshape(strip // 8, 8, piece) * gains[:, cols][None]
+                ).reshape(strip, piece).astype(BF16)
 
         if c == chunks - 1:
             own_copies[0].wait()
             own_copies[1].wait()
             own_copies[3].wait()
             for d in range(1, n_rows):
-                weight_copy(d, 0).wait()
-                weight_copy(d, 1).wait()
-        total = project(c * chunk, chunk, wkv_buf)
-        cosine, sine = tables(c * chunk, chunk)
-        here = pl.ds(mine + c * chunk, chunk)
+                wait_weights(d, 0)
+                wait_weights(d, 1)
+            own_copies[2].start()
+        if c % (half // chunk):
+            continue
+        total = project(c * chunk, half, lambda d: wkv_buf[d])
+        cosine, sine = tables(c * chunk, half)
+        here = pl.ds(mine + c * chunk, half)
         for h in range(kv_heads):
             kv[here, pl.ds(h * HEAD, HEAD)] = rotate(
                 total[:, h * HEAD : (h + 1) * HEAD], cosine, sine
@@ -195,26 +223,26 @@
 
             @pl.when(has_next)
             def _():
-                hop(0, c).start()
+                for k in reversed(range(half // chunk)):
+                    hop(0, c + k).start()
 
     relayed = [(s, c) for s in range(back - 1) for c in reversed(range(chunks))]
     last = [(back - 1, c) for c in reversed(range(chunks))] if back else []
 
     own_copies[2].wait()
     for d in range(1, n_rows):
-        weight_copy(d, 2).wait()
-    part = min(rows, 2 * chunk)
-    for step in reversed(range(rows // part)):
-        for _ in range(min(1, len(relayed))):
+        wait_weights(d, 2)
+    for step in reversed(range(rows // q_rows)):
+        if relayed:
             arrived(*relayed.pop(0))
-        total = project(step * part, part, wq_buf)
-        cosine, sine = tables(step * part, part)
+        total = project(step * q_rows, q_rows, lambda d: wq_buf[d])
+        cosine, sine = tables(step * q_rows, q_rows)
         for h in range(kv_heads):
             for g in range(group):
                 col = (h * group + g) * HEAD
                 u = rotate(total[:, col : col + HEAD], cosine, sine)
-                for t in range(part // TQ):
-                    q[step * (part // TQ) + t, h, pl.ds(g * TQ, TQ), :] = u[
+                for t in range(q_rows // TQ):
+                    q[step * (q_rows // TQ) + t, h, pl.ds(g * TQ, TQ), :] = u[
                         t * TQ : (t + 1) * TQ
                     ]
     for event in relayed:
@@ -238,12 +266,15 @@
             s = lax.dot_general(
                 q[t, h], keys, (((1,), (1,)), ((), ())), preferred_element_type=F32
             )
-            s = jnp.where(visible[None], s.reshape(group, TQ, span), -1e30)
-            p = jnp.exp2((s - jnp.max(s, axis=-1, keepdims=True)) * factor)
-            total = jnp.sum(p, axis=-1, keepdims=True)
-            mixed = jnp.dot(
-                p.astype(BF16).reshape(group * TQ, span), vals, preferred_element_type=F32
-            )
+            totals = []
+            for r in range(0, group * TQ, strip):
+                seen = visible[r % TQ : r % TQ + strip]
+                part = jnp.where(seen, s[r : r + strip], -1e30)
+                p = jnp.exp2((part - jnp.max(part, axis=-1, keepdims=True)) * factor)
+                totals.append(jnp.sum(p, axis=-1, keepdims=True))
+                probs[pl.ds(r, strip), :] = p.astype(BF16)
+            total = jnp.concatenate(totals, axis=0).reshape(group, TQ, 1)
+            mixed = jnp.dot(probs[...], vals, preferred_element_type=F32)
             mixed = (mixed.reshape(group, TQ, HEAD) / total).astype(BF16)
             for g in range(group):
                 out[pl.ds(first, TQ), pl.ds((h * group + g) * HEAD, HEAD)] = mixed[g]
@@ -273,13 +304,16 @@
         anywhere = pl.BlockSpec(memory_space=pl.ANY)
         vmem = pl.BlockSpec(memory_space=pltpu.VMEM)
         keys = (back + 1) * rows
+        span = min(keys, -(-(MOST - 1 + TQ) // TQ) * TQ)
         group = qw // kvw
         return pl.pallas_call(
-            functools.partial(kernel, n_rows, n_attn, back, chunk),
+            functools.partial(kernel, n_rows, n_attn, back, chunk, span),
             out_shape=jax.ShapeDtypeStruct((rows, qw), BF16),
             in_specs=[anywhere, vmem, anywhere, anywhere, anywhere, vmem, anywhere],
             out_specs=vmem,
             scratch_shapes=[
+                pltpu.VMEM((group * TQ, span), BF16),
+                pltpu.VMEM((8, width), F32),
                 pltpu.VMEM((rows, width), BF16),
                 pltpu.VMEM((rows, width), BF16),
                 pltpu.VMEM((n_rows, depth, 2 * kvw), BF16),
@@ -291,8 +325,8 @@
                 pltpu.VMEM((rows, TQ), jnp.int32),
                 pltpu.SemaphoreType.DMA((chunks,)),
                 pltpu.SemaphoreType.DMA((4,)),
-                pltpu.SemaphoreType.DMA((n_rows, 3)),
-                pltpu.SemaphoreType.DMA((n_rows, 3)),
+                pltpu.SemaphoreType.DMA((n_rows, 3, 4)),
+                pltpu.SemaphoreType.DMA((n_rows, 3, 4)),
                 pltpu.SemaphoreType.DMA((max(back, 1), chunks)),
                 pltpu.SemaphoreType.DMA((max(back, 1), chunks)),
             ],

time: 24.6 us -> 25.7 us (1.045)
  Pallas kernels: 22.5 us -> 23.6 us
    pallas_call x1, Pallas kernels: 22.5 us -> 23.6 us  [on_device(): pl.pallas_call(functools.partial(kernel, n_rows, n_attn, back, chunk, spa...]
where the time goes in v3:
time: 25.7 us; the launch traced here: 25.5 us
  Pallas kernels  23.6 us (92%)
  local copies, waits for them, and re-layouts  1.87 us (7%)
    pallas_call x1, Pallas kernels, on_device(): pl.pallas_call(functools.partial(kernel, n_rows, n_attn, back, chunk, spa...  23.6 us
    unnamed x1, local copies, waits for them, and re-layouts  1.87 us

profile of v3, /device:TPU:18, one launch (start us, length us, event | category | flops | bytes accessed | tf_op | source)
XLA Modules:
  0.0 25.5 jit_solution(5667376548413103981)
XLA Ops:
  0.0 23.6 %layer.1 = bf16[512,512]{1,0:T(8,128)(2,1)} custom-call(bf16[512,4096]{1,0:T(8,128)(2,1)} %tok.1, bf16[4096]{0:T(1024)(128)(2,1)} %gain.1, bf16[2048,512]{1,0:T(8,128)(2,1)} %wq.1, bf16[2048,128]{1,0:T(8,128)(2,1)} %wk.1, bf16[2048,128]{1,0:T(8,128)(2,1)} %wv.1, s32[1,2048]{1,0:T(1,128)} %docs.1, f32[2048,128]{1,0:T(8,128)} %constant.2.clone.table), custom_call_target="tpu_custom_call" | custom-call | tf_op jit(solution)/shard_map/layer/pallas_call | solution.py:309
  23.6 1.9 %copy.9 = bf16[512,512]{1,0:T(8,128)(2,1)} copy(bf16[512,512]{1,0:T(8,128)(2,1)} %layer.1) | data formatting | bytes 1048576

commit v4 on v2

--- a/solution.py
+++ b/solution.py
@@ -29,7 +29,7 @@
 def kernel(
     n_rows, n_attn, back, chunk,
     tok, gain, wq, wk, wv, docs, table, out,
-    xt, xn, wkv_buf, wq_buf, kv, q, tab, kdoc, qdoc,
+    gains, xt, xn, wkv_buf, wq_buf, kv, q, tab, kdoc, qdoc,
     tok_sem, own_sem, w_send, w_recv, kv_send, kv_recv,
 ):
     rows = tok.shape[0]
@@ -165,16 +165,30 @@
             def _():
                 hop(s + 1, c).start()
 
-    strip = 16
+    relayed = [(s, c) for s in range(back - 1) for c in reversed(range(chunks))]
+    strip, piece = 16, 256
+    width = tok.shape[1]
+    gains[...] = jnp.broadcast_to(gain[...].astype(F32).reshape(1, -1), gains.shape)
     for c in reversed(range(chunks)):
+        if c == 0 and relayed:
+            arrived(*relayed.pop(0))
         tok_copies[c].wait()
 
-        @pl.loop(0, chunk // strip, unroll=2)
+        @pl.loop(0, chunk // strip, unroll=4)
         def _(i):
             here = pl.ds(pl.multiple_of(c * chunk + i * strip, strip), strip)
-            x = xt[here, :].astype(F32)
-            scale = lax.rsqrt(jnp.mean(x * x, axis=-1, keepdims=True) + 1e-05)
-            xn[here, :] = (x * scale * gain[...].astype(F32).reshape(1, -1)).astype(BF16)
+            squares = jnp.zeros((strip, piece), F32)
+            for k in range(width // piece):
+                x = xt[here, pl.ds(k * piece, piece)].astype(F32)
+                squares = squares + x * x
+            mean_sq = jnp.sum(squares, axis=-1, keepdims=True) * (1.0 / width)
+            scale = jnp.broadcast_to(lax.rsqrt(mean_sq + 1e-05), (strip, piece))
+            for k in range(width // piece):
+                cols = pl.ds(k * piece, piece)
+                x = xt[here, cols].astype(F32) * scale
+                xn[here, cols] = (
+                    x.reshape(strip // 8, 8, piece) * gains[:, cols][None]
+                ).reshape(strip, piece).astype(BF16)
 
         if c == chunks - 1:
             own_copies[0].wait()
@@ -197,7 +211,6 @@
             def _():
                 hop(0, c).start()
 
-    relayed = [(s, c) for s in range(back - 1) for c in reversed(range(chunks))]
     last = [(back - 1, c) for c in reversed(range(chunks))] if back else []
 
     own_copies[2].wait()
@@ -280,6 +293,7 @@
             in_specs=[anywhere, vmem, anywhere, anywhere, anywhere, vmem, anywhere],
             out_specs=vmem,
             scratch_shapes=[
+                pltpu.VMEM((8, width), F32),
                 pltpu.VMEM((rows, width), BF16),
                 pltpu.VMEM((rows, width), BF16),
                 pltpu.VMEM((n_rows, depth, 2 * kvw), BF16),

time: 24.6 us -> 24.3 us (0.988)
  Pallas kernels: 22.5 us -> 22.2 us
    pallas_call x1, Pallas kernels: 22.5 us -> 22.2 us  [on_device(): pl.pallas_call(functools.partial(kernel, n_rows, n_attn, back, chunk), ou...]
where the time goes in v4:
time: 24.3 us; the launch traced here: 24.1 us
  Pallas kernels  22.2 us (91%)
  local copies, waits for them, and re-layouts  1.87 us (8%)
    pallas_call x1, Pallas kernels, on_device(): pl.pallas_call(functools.partial(kernel, n_rows, n_attn, back, chunk), ou...  22.2 us
    unnamed x1, local copies, waits for them, and re-layouts  1.87 us

profile of v4, /device:TPU:18, one launch (start us, length us, event | category | flops | bytes accessed | tf_op | source)
XLA Modules:
  0.0 24.1 jit_solution(4374512135138321318)
XLA Ops:
  0.0 22.2 %layer.1 = bf16[512,512]{1,0:T(8,128)(2,1)} custom-call(bf16[512,4096]{1,0:T(8,128)(2,1)} %tok.1, bf16[4096]{0:T(1024)(128)(2,1)} %gain.1, bf16[2048,512]{1,0:T(8,128)(2,1)} %wq.1, bf16[2048,128]{1,0:T(8,128)(2,1)} %wk.1, bf16[2048,128]{1,0:T(8,128)(2,1)} %wv.1, s32[1,2048]{1,0:T(1,128)} %docs.1, f32[2048,128]{1,0:T(8,128)} %constant.2.clone.table), custom_call_target="tpu_custom_call" | custom-call | tf_op jit(solution)/shard_map/layer/pallas_call | solution.py:290
  22.2 1.9 %copy.9 = bf16[512,512]{1,0:T(8,128)(2,1)} copy(bf16[512,512]{1,0:T(8,128)(2,1)} %layer.1) | data formatting | bytes 1048576
